TPU v7x, 256 devices: a whole 4x4x8 slice. The times are simulated.
256 devices in a mesh: ctx: 128 (over z, x, y_lo, core), head: 2 (over y_hi).
Axes of the slice: x: 4, y: 4 (y_hi: 2, y_lo: 2; y = y_hi * 2 + y_lo), z: 8, core: 2. Of those that a mesh axis runs over, the one named last changes fastest.
Arguments:
- queries: bfloat16 [16384, 2048], P('ctx', 'head'), may hold values from -12 to 12
- barred_key_rows: bfloat16 [16384, 512], P('ctx', 'head'), may hold values from -5.5 to 5.5
- barred_value_rows: bfloat16 [16384, 512], P('ctx', 'head'), may hold values from -12 to 12
- doc_start: int32 [16384], P('ctx'), may hold values from 0 to 16383, as said below
- out_weight: bfloat16 [2048, 4096], P('head'), may hold values from -0.5 to 0.5
Outputs:
- mixed: bfloat16 [16384, 4096], P('ctx', 'head')
Inputs may be any that keep to these rules, and one draw needn't show every extreme that they name: Documents are runs of consecutive positions starting at position 0; the first has exactly 8192 tokens, each other has 2048 to 8192 tokens except the last two: the final position 16383 is a document of one token, and the one before it may be shorter; doc_start of a row is the first position of its document, so it is at most pos of that row.
All inputs are finite; a program needn't handle non-finite values.
Results may differ from a plain program's by a relative error of at most 0.015.
Values may be sent and summed in bfloat16 or wider, within the bound.
A program may use at most 128 MiB of HBM per device.

v0:
```python
import math
import jax
import jax.numpy as jnp
from jax import lax
from jax.sharding import PartitionSpec as P

HEAD_SIZE = 128
STRIPE = 64
MASKED_SCORE = -1e30


def positions(row_index, tok_dev, cycle_size):
    shard_index = row_index // tok_dev
    within = row_index % tok_dev
    return (within // STRIPE * cycle_size + shard_index) * STRIPE + within % STRIPE


def attend(state, query_block, key_block, value_block, query_pos, query_doc, key_pos, score_scale):
    running_max, running_sum, weighted = state
    scores = (
        jnp.einsum("tkgd,nkd->kgtn", query_block, key_block, preferred_element_type=jnp.float32)
        * score_scale
    )
    visible = (query_doc[:, None] <= key_pos[None, :]) & (key_pos[None, :] <= query_pos[:, None])
    scores = jnp.where(visible, scores, MASKED_SCORE)
    new_max = jnp.maximum(running_max, jnp.max(scores, axis=-1))
    weights = jnp.where(visible, jnp.exp(scores - new_max[..., None]), 0.0).astype(jnp.bfloat16)
    shrink = jnp.exp(running_max - new_max)
    running_sum = running_sum * shrink + jnp.sum(weights.astype(jnp.float32), axis=-1)
    weighted = weighted * shrink[..., None] + jnp.einsum(
        "kgtn,nkd->kgtd", weights, value_block, preferred_element_type=jnp.float32
    )
    return (new_max, running_sum, weighted)


def local(queries, barred_key_rows, barred_value_rows, doc_start, out_weight):
    tok_dev = queries.shape[0]
    key_heads = barred_key_rows.shape[1] // HEAD_SIZE
    heads_per_group = queries.shape[1] // barred_key_rows.shape[1]
    cycle_size = lax.axis_size("ctx")
    score_scale = 1.0 / math.sqrt(HEAD_SIZE)
    own_rows = lax.axis_index("ctx") * tok_dev + jnp.arange(tok_dev, dtype=jnp.int32)
    query_pos = positions(own_rows, tok_dev, cycle_size)
    query_split = queries.reshape(tok_dev, key_heads, heads_per_group, HEAD_SIZE)
    start_state = (
        jnp.full((key_heads, heads_per_group, tok_dev), MASKED_SCORE, jnp.float32),
        jnp.zeros((key_heads, heads_per_group, tok_dev), jnp.float32),
        jnp.zeros((key_heads, heads_per_group, tok_dev, HEAD_SIZE), jnp.float32),
    )
    state = start_state
    key_piece = lax.all_gather(barred_key_rows, "ctx", axis=0, tiled=True)
    value_piece = lax.all_gather(barred_value_rows, "ctx", axis=0, tiled=True)
    fetched_rows = key_piece.shape[0]
    shards = fetched_rows // tok_dev
    per_block = 4
    block_count = shards // per_block
    row_index = jnp.arange(fetched_rows, dtype=jnp.int32)
    key_pos_all = positions(row_index, tok_dev, cycle_size)
    key_blocks = key_piece.reshape(block_count, per_block * tok_dev, key_heads, HEAD_SIZE)
    value_blocks = value_piece.reshape(block_count, per_block * tok_dev, key_heads, HEAD_SIZE)
    pos_blocks = key_pos_all.reshape(block_count, per_block * tok_dev)

    def one_block(carried, block_data):
        key_block, value_block, pos_block = block_data
        return (
            attend(
                carried,
                query_split,
                key_block,
                value_block,
                query_pos,
                doc_start,
                pos_block,
                score_scale,
            ),
            None,
        )

    state, unused = lax.scan(one_block, state, (key_blocks, value_blocks, pos_blocks))
    running_max, running_sum, weighted = state
    scaled = weighted / running_sum[..., None]
    attn = (
        jnp.transpose(scaled, (2, 0, 1, 3))
        .reshape(tok_dev, key_heads * heads_per_group * HEAD_SIZE)
        .astype(jnp.bfloat16)
    )
    partial_out = jnp.dot(attn, out_weight, preferred_element_type=jnp.float32)
    return lax.psum_scatter(
        partial_out.astype(jnp.bfloat16), "head", scatter_dimension=1, tiled=True
    )


def solution(mesh):
    placed = (P("ctx", "head"), P("ctx", "head"), P("ctx", "head"), P("ctx"), P("head", None))
    return jax.shard_map(
        local, mesh=mesh, in_specs=placed, out_specs=P("ctx", "head"), check_vma=False
    )
```

profile of v0, /device:TPU:1, one launch (start us, length us, event | category | flops | bytes accessed | tf_op | source)
XLA Modules:
  0.0 621.1 jit_solution(1597774503833811170)
XLA Ops:
  9.5 223.9 %all-gather.3.cloned.1.call-done = bf16[16384,256]{1,0:T(8,128)(2,1)} async-done(((bf16[128,256]{1,0:T(8,128)(2,1)}), bf16[16384,256]{1,0:T(8,128)(2,1)}) %all-gather.3.cloned.1.call-update) | async-done | bytes 8388624 | tf_op jit(solution)/shard_map/all_gather | solution.py:51
  233.4 12.5 %reshape.30 = bf16[32,512,2,128]{3,2,1,0:T(2,128)(2,1)} reshape(bf16[16384,256]{1,0:T(8,128)(2,1)} %all-gather.3.cloned.1.call-done) | data formatting | bytes 16777216 | tf_op jit(solution)/shard_map/reshape | solution.py:59
  246.0 208.7 %all-gather.5.cloned.1.call-done = bf16[16384,256]{1,0:T(8,128)(2,1)} async-done(((bf16[128,256]{1,0:T(8,128)(2,1)}), bf16[16384,256]{1,0:T(8,128)(2,1)}) %all-gather.5.cloned.1.call-update) | async-done | bytes 8388624 | tf_op jit(solution)/shard_map/all_gather | solution.py:52
  454.6 12.5 %reshape.31 = bf16[32,512,2,128]{3,2,1,0:T(2,128)(2,1)} reshape(bf16[16384,256]{1,0:T(8,128)(2,1)} %all-gather.5.cloned.1.call-done) | data formatting | bytes 16777216 | tf_op jit(solution)/shard_map/reshape | solution.py:60
  467.2 115.4 %while.15 = (s32[]{:T(128)}, f32[2,4,128]{2,1,0:T(4,128)S(1)}, f32[2,4,128]{2,1,0:T(4,128)S(1)}, f32[2,4,128,128]{3,2,1,0:T(8,128)S(1)}, s32[128]{0:T(128)S(1)},...) while((s32[]{:T(128)}, f32[2,4,128]{2,1,0:T(4,128)S(1)}, ...), condition=%wide.region_3.4_spmd.clone, body=%wide.region_0.3_spmd.clone.sunk | while | flops 276900224 | bytes 9510541 | solution.py:79
  467.3 1.4 constant_dynamic-slice_fusion.6
  470.9 1.4 constant_dynamic-slice_fusion.6
  474.6 1.4 constant_dynamic-slice_fusion.6
  478.2 1.4 constant_dynamic-slice_fusion.6
  481.8 1.4 constant_dynamic-slice_fusion.6
  485.4 1.4 constant_dynamic-slice_fusion.6
  489.0 1.4 constant_dynamic-slice_fusion.6
  492.6 1.4 constant_dynamic-slice_fusion.6
  496.2 1.4 constant_dynamic-slice_fusion.6
  499.8 1.4 constant_dynamic-slice_fusion.6
  503.4 1.4 constant_dynamic-slice_fusion.6
  507.0 1.4 constant_dynamic-slice_fusion.6
  510.6 1.4 constant_dynamic-slice_fusion.6
  514.2 1.4 constant_dynamic-slice_fusion.6
  517.8 1.4 constant_dynamic-slice_fusion.6
  521.4 1.4 constant_dynamic-slice_fusion.6
  525.0 1.4 constant_dynamic-slice_fusion.6
  528.7 1.4 constant_dynamic-slice_fusion.6
  532.3 1.4 constant_dynamic-slice_fusion.6
  535.9 1.4 constant_dynamic-slice_fusion.6
  539.5 1.4 constant_dynamic-slice_fusion.6
  550.3 1.4 constant_dynamic-slice_fusion.6
  553.9 1.4 constant_dynamic-slice_fusion.6
  557.5 1.4 constant_dynamic-slice_fusion.6
  564.7 1.4 constant_dynamic-slice_fusion.6
  582.8 5.7 convolution_convert_fusion
  588.5 26.0 %reduce-scatter.2.cloned.1.call-done = bf16[128,2048]{1,0:T(8,128)(2,1)} async-done(((bf16[128,4096]{1,0:T(8,128)(2,1)}), bf16[128,2048]{1,0:T(8,128)(2,1)}) %reduce-scatter.2.cloned.1.call-update) | async-done | bytes 524304 | tf_op jit(solution)/shard_map/reduce_scatter | solution.py:88
  (311 shorter events, 81.6 us)
Async XLA Ops:
  6.5 226.9 %all-gather.3.cloned.1.call-start = ((), (), s32[]{:S(2)}) async-start(), calls=%async_computation.1 | async-start | bytes 8454144 | tf_op jit(solution)/shard_map/all_gather | solution.py:51
  7.3 447.4 %all-gather.5.cloned.1.call-start = ((), (), s32[]{:S(2)}) async-start(), calls=%async_computation.2 | async-start | bytes 8454144 | tf_op jit(solution)/shard_map/all_gather | solution.py:52
  8.0 606.5 %reduce-scatter.2.cloned.1.call-start = ((), (), s32[]{:S(2)}) async-start(), calls=%async_computation.3 | async-start | bytes 1572864 | tf_op jit(solution)/shard_map/reduce_scatter | solution.py:88
  246.0 221.2 %copy-start = (s32[128]{0:T(128)S(1)}, s32[128]{0:T(128)}, u32[]{:S(2)}) copy-start(s32[128]{0:T(128)} %param.10) | copy-start | bytes 1540
Sparse Core Ops, SparseCore 0:
  9.2 224.1 all-gather.2
  235.3 219.2 all-gather.4
  588.6 25.8 reduce-scatter.1
where the time goes:
time: 622 us; the launch traced here: 621 us
  waiting for transfers between devices  460 us (74%)
  local copies, waits for them, and re-layouts  71.7 us (12%)
  matrix products  51.2 us (8%)
  other arithmetic  22.9 us (4%)
  between operations  13.2 us (2%)
    all_gather x1, waiting for transfers between devices, local(): key_piece = lax.all_gather(barred_key_rows, 'ctx', axis=0, tiled=True)  224 us
    all_gather x1, waiting for transfers between devices, local(): value_piece = lax.all_gather(barred_value_rows, 'ctx', axis=0, tiled=True)  209 us
    dynamic_slice x64, local copies, waits for them, and re-layouts, local(): lax.scan(one_block, state, (key_blocks, value_blocks, pos_blocks))  45 us
    dot_general x32, matrix products, attend(): jnp.einsum('kgtn,nkd->kgtd', weights, value_block, preferred_element_type...  30.7 us
    reduce_scatter x1, waiting for transfers between devices, local(): lax.psum_scatter(partial_out.astype(jnp.bfloat16), 'head', scatter_dimens...  26 us
    reduce_sum x32, other arithmetic, attend(): jnp.sum(weights.astype(jnp.float32), axis=-1)  16.7 us
    dot_general x32, matrix products, attend(): jnp.einsum('tkgd,nkd->kgtn', query_block, key_block, preferred_element_ty...  14.9 us
    reshape x1, local copies, waits for them, and re-layouts, local(): key_piece.reshape(block_count, per_block * tok_dev, key_heads, HEAD_SIZE)  12.5 us
  transfers between devices with their start and end apart: 3, of which 3 were waited for; matrix products, arithmetic and copies ran while one was open for 2% of the time, Pallas kernels for 0%

commit v1 on v0

--- a/solution.py
+++ b/solution.py
@@ -49,7 +49,10 @@
     )
     state = start_state
     key_piece = lax.all_gather(barred_key_rows, "ctx", axis=0, tiled=True)
-    value_piece = lax.all_gather(barred_value_rows, "ctx", axis=0, tiled=True)
+    size = lax.axis_size("ctx")
+    parts = jnp.stack([barred_value_rows for _ in range(size)])
+    parts = lax.all_to_all(parts, "ctx", split_axis=0, concat_axis=0)
+    value_piece = jnp.concatenate(parts, axis=0)
     fetched_rows = key_piece.shape[0]
     shards = fetched_rows // tok_dev
     per_block = 4

time: 622 us -> 511 us (0.82)
  waiting for transfers between devices: 460 us -> 276 us
  matrix products: 51.2 us -> 81 us
  local copies, waits for them, and re-layouts: 71.7 us -> 96.9 us
  starting transfers between devices: 0.08 us -> 15.6 us
    all_gather x1 -> x0, waiting for transfers between devices: 209 us -> none  [local(): value_piece = lax.all_gather(barred_value_rows, 'ctx', axis=0, tiled=True)]
    all_to_all x0 -> x1, waiting for transfers between devices: none -> 207 us  [local(): parts = lax.all_to_all(parts, 'ctx', split_axis=0, concat_axis=0)]
    all_gather x1, waiting for transfers between devices: 224 us -> 35.8 us  [local(): key_piece = lax.all_gather(barred_key_rows, 'ctx', axis=0, tiled=True)]
    dot_general x32, matrix products: 30.7 us -> 60.5 us  [attend(): jnp.einsum('kgtn,nkd->kgtd', weights, value_block, preferred_element_type...]
    another operation x0 -> x2, local copies, waits for them, and re-layouts: none -> 19.3 us  [the longest x1 14 us: local(): value_piece.reshape(block_count, per_block * tok_dev, key_heads, HEAD_SIZE)]
    all_to_all x0 -> x1, starting transfers between devices: none -> 15.4 us  [local(): parts = lax.all_to_all(parts, 'ctx', split_axis=0, concat_axis=0)]
    unnamed x4 -> x8, local copies, waits for them, and re-layouts: 1.3 us -> 16 us
    reshape x1 -> x0, local copies, waits for them, and re-layouts: 12.5 us -> none  [local(): value_piece.reshape(block_count, per_block * tok_dev, key_heads, HEAD_SIZE)]
  transfers between devices with their start and end apart: 3 -> 3, of which waited for: 3 -> 3; matrix products, arithmetic and copies ran while one was open for 2% -> 8% of each run, Pallas kernels for 0% -> 0%
where the time goes in v1:
time: 511 us; the launch traced here: 508 us
  waiting for transfers between devices  276 us (54%)
  local copies, waits for them, and re-layouts  96.9 us (19%)
  matrix products  81 us (16%)
  other arithmetic  22.9 us (4%)
  starting transfers between devices  15.6 us (3%)
  between operations  13.5 us (3%)
    all_to_all x1, waiting for transfers between devices, local(): parts = lax.all_to_all(parts, 'ctx', split_axis=0, concat_axis=0)  207 us
    dot_general x32, matrix products, attend(): jnp.einsum('kgtn,nkd->kgtd', weights, value_block, preferred_element_type...  60.5 us
    dynamic_slice x64, local copies, waits for them, and re-layouts, local(): lax.scan(one_block, state, (key_blocks, value_blocks, pos_blocks))  36.7 us
    all_gather x1, waiting for transfers between devices, local(): key_piece = lax.all_gather(barred_key_rows, 'ctx', axis=0, tiled=True)  35.8 us
    reduce_scatter x1, waiting for transfers between devices, local(): lax.psum_scatter(partial_out.astype(jnp.bfloat16), 'head', scatter_dimens...  31.9 us
    reduce_sum x32, other arithmetic, attend(): jnp.sum(weights.astype(jnp.float32), axis=-1)  16.7 us
    unnamed x8, local copies, waits for them, and re-layouts  16 us
    all_to_all x1, starting transfers between devices, local(): parts = lax.all_to_all(parts, 'ctx', split_axis=0, concat_axis=0)  15.4 us
  transfers between devices with their start and end apart: 3, of which 3 were waited for; matrix products, arithmetic and copies ran while one was open for 8% of the time, Pallas kernels for 0%

profile of v1, /device:TPU:1, one launch (start us, length us, event | category | flops | bytes accessed | tf_op | source)
XLA Modules:
  0.0 507.9 jit_solution(9622242502170716176)
XLA Ops:
  7.5 5.3 %stack.2 = bf16[128,128,256]{1,2,0:T(8,128)(2,1)} broadcast(bf16[128,256]{0,1:T(8,128)(2,1)S(1)} %copy.18), dimensions={1,2} | broadcast | bytes 8454144 | tf_op jit(solution)/shard_map/stack | solution.py:53
  12.8 15.4 %all-to-all-start = ((bf16[128,128,256]{1,2,0:T(8,128)(2,1)}), bf16[128,128,256]{1,2,0:T(8,128)(2,1)}, u32[]{:S(2)}, u32[]{:S(2)}) async-start(bf16[128,128,256]{1,2,0:T(8,128)(2,1)} %stack.2), calls=%async_computation | async-start | bytes 16777216 | tf_op jit(solution)/shard_map/all_to_all | solution.py:54
  29.7 207.4 %all-to-all-done = bf16[128,128,256]{1,2,0:T(8,128)(2,1)} async-done(((bf16[128,128,256]{1,2,0:T(8,128)(2,1)}), bf16[128,128,256]{1,2,0:T(8,128)(2,1)}, u32[]{:S(2)}, u32[]{:S(2)}) %all-to-all-start) | async-done | bytes 8388640 | tf_op jit(solution)/shard_map/all_to_all | solution.py:54
  237.1 12.0 %copy.19 = bf16[128,128,256]{1,0,2:T(8,128)(2,1)} copy(bf16[128,128,256]{1,2,0:T(8,128)(2,1)} %all-to-all-done) | data formatting | bytes 16777216 | tf_op jit(solution)/shard_map/all_to_all | solution.py:54
  249.1 14.0 %reshape_reshape.3 = bf16[32,512,2,128]{1,0,3,2:T(8,128)(2,1)} reshape(bf16[128,128,256]{1,0,2:T(8,128)(2,1)} %copy.19) | data formatting | bytes 16777216 | tf_op jit(solution)/shard_map/reshape;reshape | solution.py:63
  263.1 14.7 %copy.22 = bf16[32,512,2,128]{3,1,2,0:T(8,128)(2,1)} copy(bf16[32,512,2,128]{1,0,3,2:T(8,128)(2,1)} %reshape_reshape.3) | data formatting | bytes 16777216
  277.8 35.8 %all-gather.2.cloned.1.call-done = bf16[16384,256]{1,0:T(8,128)(2,1)} async-done(((bf16[128,256]{1,0:T(8,128)(2,1)}), bf16[16384,256]{1,0:T(8,128)(2,1)}) %all-gather.2.cloned.1.call-update) | async-done | bytes 8388624 | tf_op jit(solution)/shard_map/all_gather | solution.py:51
  313.6 12.6 %reshape.28 = bf16[32,512,2,128]{3,2,1,0:T(2,128)(2,1)} reshape(bf16[16384,256]{1,0:T(8,128)(2,1)} %all-gather.2.cloned.1.call-done) | data formatting | bytes 16777216 | tf_op jit(solution)/shard_map/reshape | solution.py:62
  326.2 137.0 %while.15 = (s32[]{:T(128)}, f32[2,4,128]{2,1,0:T(4,128)S(1)}, f32[2,4,128]{2,1,0:T(4,128)S(1)}, f32[2,4,128,128]{3,2,1,0:T(8,128)S(1)}, s32[128]{0:T(128)S(1)},...) while((s32[]{:T(128)}, f32[2,4,128]{2,1,0:T(4,128)S(1)}, ...), condition=%wide.region_3.4_spmd.clone, body=%wide.region_0.3_spmd.clone.sunk | while | flops 276900224 | bytes 8986765 | solution.py:82
  328.5 1.9 convolution_add_fusion.2
  332.8 1.9 convolution_add_fusion.2
  337.1 1.9 convolution_add_fusion.2
  341.4 1.9 convolution_add_fusion.2
  345.6 1.9 convolution_add_fusion.2
  349.9 1.9 convolution_add_fusion.2
  354.2 1.9 convolution_add_fusion.2
  358.5 1.9 convolution_add_fusion.2
  362.8 1.9 convolution_add_fusion.2
  367.1 1.9 convolution_add_fusion.2
  375.6 1.9 convolution_add_fusion.2
  384.2 1.9 convolution_add_fusion.2
  392.7 1.9 convolution_add_fusion.2
  401.3 1.9 convolution_add_fusion.2
  409.9 1.9 convolution_add_fusion.2
  418.4 1.9 convolution_add_fusion.2
  427.0 1.9 convolution_add_fusion.2
  435.6 1.9 convolution_add_fusion.2
  444.1 1.9 convolution_add_fusion.2
  452.7 1.9 convolution_add_fusion.2
  461.3 1.9 convolution_add_fusion.2
  463.4 5.6 %convolution_convert_fusion = bf16[128,4096]{1,0:T(8,128)(2,1)} fusion(bf16[128,1024]{0,1:T(8,128)(2,1)S(1)} %bitcast.47, bf16[1024,4096]{1,0:T(8,128)(2,1)} %param.11), kind=kOutput, calls=%fused_computation.30 | convolution fusion | flops 1074266112 | bytes 9699328 | tf_op jit(solution)/shard_map/dot_general | solution.py:90
  469.1 31.9 %reduce-scatter.2.cloned.1.call-done = bf16[128,2048]{1,0:T(8,128)(2,1)} async-done(((bf16[128,4096]{1,0:T(8,128)(2,1)}), bf16[128,2048]{1,0:T(8,128)(2,1)}) %reduce-scatter.2.cloned.1.call-update) | async-done | bytes 524304 | tf_op jit(solution)/shard_map/reduce_scatter | solution.py:91
  (316 shorter events, 97.8 us)
Async XLA Ops:
  12.8 16.4 %copy-start = (bf16[128,1024]{1,0:T(8,128)(2,1)S(1)}, bf16[128,1024]{1,0:T(8,128)(2,1)}, u32[]{:S(2)}) copy-start(bf16[128,1024]{1,0:T(8,128)(2,1)} %param.7) | copy-start | bytes 786436
  12.8 224.3 %all-to-all-start = ((bf16[128,128,256]{1,2,0:T(8,128)(2,1)}), bf16[128,128,256]{1,2,0:T(8,128)(2,1)}, u32[]{:S(2)}, u32[]{:S(2)}) async-start(bf16[128,128,256]{1,2,0:T(8,128)(2,1)} %stack.2), calls=%async_computation | async-start | bytes 16777216 | tf_op jit(solution)/shard_map/all_to_all | solution.py:54
  28.2 285.4 %all-gather.2.cloned.1.call-start = ((), (), s32[]{:S(2)}) async-start(), calls=%async_computation.2 | async-start | bytes 8454144 | tf_op jit(solution)/shard_map/all_gather | solution.py:51
  28.9 472.1 %reduce-scatter.2.cloned.1.call-start = ((), (), s32[]{:S(2)}) async-start(), calls=%async_computation.3 | async-start | bytes 1572864 | tf_op jit(solution)/shard_map/reduce_scatter | solution.py:91
  277.8 48.3 %copy-start.1 = (s32[128]{0:T(128)S(1)}, s32[128]{0:T(128)}, u32[]{:S(2)}) copy-start(s32[128]{0:T(128)} %param.10) | copy-start | bytes 1540
Sparse Core Ops, SparseCore 0:
  30.9 282.6 all-gather.1
  469.2 31.7 reduce-scatter.1
